TPU v7x, 256 devices: a whole 4x4x8 slice. The times are simulated.
256 devices in a mesh: expert: 64 (over y, z, core), dp: 4 (over x).
Axes of the slice: x: 4, y: 4, z: 8, core: 2. Of those that a mesh axis runs over, the one named last changes fastest.
Arguments:
- tokens: bfloat16 [32768, 1440], P(('expert', 'dp')), may hold values from -6 to 6
- routes: int32 [32768, 4], P(('expert', 'dp')), may hold values from 0 to 63, as said below
- gate_fixed: int32 [32768, 4], P(('expert', 'dp')), may hold values from 4096 to 65535
- counts: int32 [256], P(('expert', 'dp')), may hold values from 32 to 128, as said below
- replica_plan: int32 [8], replicated, may hold values from 0 to 63, as said below
- weight_in: bfloat16 [64, 1440, 1440], P('expert', None, 'dp'), may hold values from -0.15625 to 0.15625
- weight_out: bfloat16 [64, 1440, 1440], P('expert', 'dp'), may hold values from -0.15625 to 0.15625
- cotangent: bfloat16 [32768, 1440], P(('expert', 'dp')), may hold values from -0.59765625 to 0.59765625
Outputs:
- layer_output: bfloat16 [32768, 1440], P(('expert', 'dp'))
- input_grads: bfloat16 [32768, 1440], P(('expert', 'dp'))
- weight_in_grad: bfloat16 [64, 1440, 1440], P('expert', None, 'dp')
- weight_out_grad: bfloat16 [64, 1440, 1440], P('expert', 'dp')
Inputs may be any that keep to these rules, and one draw needn't show every extreme that they name: `routes`: each row names 4 different experts. `replica_plan`: 8 different experts, among them 0, 31, 32 and 63, in any order. `counts`: some device has 128 live tokens in every draw.
All inputs are finite; a program needn't handle non-finite values.
Results may differ from a plain program's by a relative error of at most 0.0064.
Values may be sent and summed in bfloat16 or wider, within the bound.
No kernel may reach another device: no remote copies, remote signals or barrier semaphores. Data moves between devices by JAX's collectives and lax.ppermute only.
A program may use at most 128 MiB of HBM per device.

v0:
```python
import jax
import jax.numpy as jnp
from jax import lax
from jax.sharding import PartitionSpec as P


def shifted(value, axis, steps):
    count = lax.axis_size(axis)
    pairs = [(source, (source + steps) % count) for source in range(count)]
    return lax.ppermute(value, axis, pairs)


def activate(values):
    return values * jax.nn.sigmoid(1.702 * values)


def derivative(values):
    sigmoid_value = jax.nn.sigmoid(1.702 * values)
    return sigmoid_value + 1.702 * values * sigmoid_value * (1.0 - sigmoid_value)


def slot_tables(routes, live_count, frequent_indicator, experts, capacity, spare_slots):
    token_count, top_count = routes.shape
    slot_width = capacity + spare_slots
    active = (jnp.arange(token_count, dtype=jnp.int32) < live_count).astype(jnp.int32)
    flattened = routes.reshape(-1)
    active_flat = jnp.repeat(active, top_count, total_repeat_length=token_count * top_count)
    same_expert = (flattened[:, None] == jnp.arange(experts, dtype=jnp.int32)[None, :]).astype(
        jnp.int32
    )
    matches = same_expert * active_flat[:, None]
    before = jnp.cumsum(matches, axis=0) - matches
    position = jnp.sum(before * matches, axis=1)
    hot_route = jnp.sum(same_expert * frequent_indicator[None, :], axis=1)
    keep_route = (active_flat > 0) & (position < capacity + spare_slots * hot_route)
    target_block = jnp.where(position < capacity, flattened, (flattened + experts // 2) % experts)
    slot_index = jnp.where(keep_route, target_block * slot_width + position, experts * slot_width)
    source = jnp.full((experts * slot_width + 1,), -1, jnp.int32)
    source = source.at[slot_index].set(jnp.arange(token_count * top_count, dtype=jnp.int32))
    return (slot_index, source[: experts * slot_width])


def gather_back(returned, slot_index, features):
    flattened = returned.reshape(-1, features)
    padded = jnp.concatenate([flattened, jnp.zeros((1, features), flattened.dtype)], axis=0)
    return padded[slot_index].astype(jnp.float32)


def slot_products(stacked, own_weight, copy_weight, dims, capacity, amount):
    width = stacked.shape[2]
    own_part = stacked[:, :capacity].reshape(-1, width)
    copy_part = stacked[:, capacity:].reshape(-1, width)
    own_term = lax.dot_general(own_part, own_weight, dims, preferred_element_type=jnp.float32)
    copy_term = lax.dot_general(copy_part, copy_weight, dims, preferred_element_type=jnp.float32)
    return jnp.concatenate(
        [
            own_term.reshape(amount, capacity, -1),
            copy_term.reshape(amount, stacked.shape[1] - capacity, -1),
        ],
        axis=1,
    )


def on_device(tokens, routes, gate_fixed, counts, replica_plan, weight_in, weight_out, cotangent):
    token_count, features = tokens.shape
    top_count = routes.shape[1]
    groups = lax.axis_size("expert")
    experts = groups * weight_in.shape[0]
    capacity = 3 * token_count * top_count // (8 * experts)
    spare_slots = capacity // 2
    slot_width = capacity + spare_slots
    contract_first = (((0,), (0,)), ((), ()))
    contract_last = (((1,), (1,)), ((), ()))
    contract_plain = (((1,), (0,)), ((), ()))
    frequent_indicator = jnp.sum(
        (replica_plan[:, None] == jnp.arange(experts, dtype=jnp.int32)[None, :]).astype(jnp.int32),
        axis=0,
    )
    slot_index, source = slot_tables(
        routes, counts[0], frequent_indicator, experts, capacity, spare_slots
    )
    filled = (source >= 0)[:, None]
    route_ids = jnp.maximum(source, 0)
    token_ids = route_ids // top_count
    scales = gate_fixed.reshape(-1).astype(jnp.float32) / 65536.0
    sent_rows = jnp.where(filled, tokens[token_ids], jnp.zeros((), jnp.bfloat16)).reshape(
        experts, slot_width, features
    )
    grad_rows = jnp.where(
        filled, scales[route_ids][:, None] * cotangent[token_ids].astype(jnp.float32), 0.0
    )
    grad_rows = grad_rows.astype(jnp.bfloat16).reshape(experts, slot_width, features)
    slab_in, slab_out = shifted((weight_in, weight_out), "expert", groups // 2)
    w_first = weight_in[0]
    w_second = weight_out[0]
    copy_first = slab_in[0]
    copy_second = slab_out[0]
    inbound = lax.all_to_all(sent_rows, "expert", split_axis=0, concat_axis=0, tiled=True)
    all_in = lax.all_gather(inbound, "dp", axis=0, tiled=True)
    blocks = all_in.shape[0]
    own_rows = all_in[:, :capacity].reshape(-1, features)
    copy_rows = all_in[:, capacity:].reshape(-1, features)
    own_pre = jnp.dot(own_rows, w_first, preferred_element_type=jnp.float32)
    copy_pre = jnp.dot(copy_rows, copy_first, preferred_element_type=jnp.float32)
    own_act = activate(own_pre).astype(jnp.bfloat16)
    copy_act = activate(copy_pre).astype(jnp.bfloat16)
    hidden_share = own_act.shape[1]
    act_all = jnp.concatenate(
        [
            own_act.reshape(blocks, capacity, hidden_share),
            copy_act.reshape(blocks, spare_slots, hidden_share),
        ],
        axis=1,
    )
    outputs = lax.psum_scatter(
        slot_products(
            act_all, w_second, copy_second, contract_plain, capacity, groups * lax.axis_size("dp")
        ),
        "dp",
        scatter_dimension=0,
        tiled=True,
    ).astype(jnp.bfloat16)
    returned = lax.all_to_all(outputs, "expert", split_axis=0, concat_axis=0, tiled=True)
    inbound_grad = lax.all_to_all(grad_rows, "expert", split_axis=0, concat_axis=0, tiled=True)
    all_grad = lax.all_gather(inbound_grad, "dp", axis=0, tiled=True)
    own_grad = all_grad[:, :capacity].reshape(-1, features)
    copy_grad = all_grad[:, capacity:].reshape(-1, features)
    own_act_grad = lax.dot_general(
        own_grad, w_second, contract_last, preferred_element_type=jnp.float32
    )
    copy_act_grad = lax.dot_general(
        copy_grad, copy_second, contract_last, preferred_element_type=jnp.float32
    )
    own_pre_grad = (own_act_grad * derivative(own_pre)).astype(jnp.bfloat16)
    copy_pre_grad = (copy_act_grad * derivative(copy_pre)).astype(jnp.bfloat16)
    pre_all = jnp.concatenate(
        [
            own_pre_grad.reshape(blocks, capacity, hidden_share),
            copy_pre_grad.reshape(blocks, spare_slots, hidden_share),
        ],
        axis=1,
    )
    input_rows = lax.psum_scatter(
        slot_products(
            pre_all, w_first, copy_first, contract_last, capacity, groups * lax.axis_size("dp")
        ),
        "dp",
        scatter_dimension=0,
        tiled=True,
    ).astype(jnp.bfloat16)
    copy_term_second = lax.dot_general(
        copy_act, copy_grad, contract_first, preferred_element_type=jnp.float32
    )
    copy_term_first = lax.dot_general(
        copy_rows, copy_pre_grad, contract_first, preferred_element_type=jnp.float32
    )
    home_second, home_first = (
        shifted(copy_term_second.astype(jnp.bfloat16), "expert", groups // 2).astype(
            copy_term_second.dtype
        ),
        shifted(copy_term_first.astype(jnp.bfloat16), "expert", groups // 2).astype(
            copy_term_first.dtype
        ),
    )
    grad_second = (
        lax.dot_general(own_act, own_grad, contract_first, preferred_element_type=jnp.float32)
        + home_second
    )
    grad_first = (
        lax.dot_general(own_rows, own_pre_grad, contract_first, preferred_element_type=jnp.float32)
        + home_first
    )
    weight_out_grad = grad_second.astype(jnp.bfloat16)[None]
    weight_in_grad = grad_first.astype(jnp.bfloat16)[None]
    returned_grad = lax.all_to_all(input_rows, "expert", split_axis=0, concat_axis=0, tiled=True)
    picked = gather_back(returned, slot_index, features) * scales[:, None]
    layer_output = jnp.sum(picked.reshape(token_count, top_count, features), axis=1).astype(
        jnp.bfloat16
    )
    picked_grad = gather_back(returned_grad, slot_index, features)
    input_grads = jnp.sum(picked_grad.reshape(token_count, top_count, features), axis=1).astype(
        jnp.bfloat16
    )
    return (layer_output, input_grads, weight_in_grad, weight_out_grad)


def solution(mesh):
    return jax.shard_map(
        on_device,
        mesh=mesh,
        in_specs=(
            P(("expert", "dp"), None),
            P(("expert", "dp"), None),
            P(("expert", "dp"), None),
            P(("expert", "dp")),
            P(),
            P("expert", None, "dp"),
            P("expert", "dp", None),
            P(("expert", "dp"), None),
        ),
        out_specs=(
            P(("expert", "dp"), None),
            P(("expert", "dp"), None),
            P("expert", None, "dp"),
            P("expert", "dp", None),
        ),
        check_vma=False,
    )
```

profile of v0, /device:TPU:1, one launch (start us, length us, event | category | flops | bytes accessed | tf_op | source)
XLA Modules:
  0.0 530.6 jit_solution(11869775184831770626)
XLA Ops:
  8.7 3.3 gather_fusion
  12.8 1.2 reduce-window.14
  14.4 2.4 scatter_custom_fusion
  17.3 1.9 gather_fusion.3
  19.6 1.3 gather_fusion.4
  21.8 36.2 %all_to_all.20 = bf16[64,4,1440]{2,1,0:T(4,128)(2,1)} all-to-all(bf16[64,4,1440]{2,1,0:T(4,128)(2,1)S(1)} %select_convert_fusion), channel_id=1, replica_groups=mesh['expert'=64,'dp'=4] {'expert'}, dimensions={0} | all-to-all | bytes 1474560 | tf_op jit(solution)/shard_map/all_to_all | solution.py:124
  58.2 1.3 gather_fusion.1
  60.1 29.1 %all_to_all.21 = bf16[64,4,1440]{2,1,0:T(4,128)(2,1)} all-to-all(bf16[64,4,1440]{2,1,0:T(4,128)(2,1)S(1)} %broadcast_select_fusion), channel_id=1, replica_groups=mesh['expert'=64,'dp'=4] {'expert'}, dimensions={0} | all-to-all | bytes 1474560 | tf_op jit(solution)/shard_map/all_to_all | solution.py:98
  89.2 2.9 collective-permute-start
  93.5 3.5 all-gather.5.cloned.1.call-done
  97.1 3.6 slice.60
  100.7 3.3 copy.76
  104.0 37.2 %all-gather.3.cloned.1.call-done = bf16[256,4,1440]{2,1,0:T(4,128)(2,1)} async-done(((bf16[64,4,1440]{2,1,0:T(4,128)(2,1)}), bf16[256,4,1440]{2,1,0:T(4,128)(2,1)}) %all-gather.3.cloned.1.call-update) | async-done | bytes 2949136 | tf_op jit(solution)/shard_map/all_gather | solution.py:99
  141.2 4.9 slice.58
  146.1 4.6 copy.75
  150.7 4.1 reshape.318
  154.8 5.4 %reshape.314 = bf16[768,1440]{1,0:T(8,128)(2,1)S(1)} reshape(bf16[256,3,1440]{2,1,0:T(4,128)(2,1)} %bitcast.86) | data formatting | bytes 4423680 | tf_op jit(solution)/shard_map/reshape | solution.py:101
  160.2 3.3 multiply_convert_fusion
  163.6 2.6 fusion
  168.4 1.8 fusion.11
  170.3 2.7 fusion.6
  172.9 1.7 fusion.1
  174.7 1.8 convolution_bitcast_fusion
  176.5 2.9 pad_maximum_fusion.1
  179.4 7.9 %copy.70 = f32[256,4,1440]{2,1,0:T(4,128)} copy(f32[256,4,1440]{0,2,1:T(8,128)} %pad_maximum_fusion.1) | data formatting | bytes 11796480 | tf_op jit(solution)/shard_map/concatenate | solution.py:55
  187.3 2.6 fusion.4
  189.9 1.9 convolution_bitcast_fusion.1
  191.8 2.9 pad_maximum_fusion
  194.7 7.8 %copy.63 = f32[256,4,1440]{2,1,0:T(4,128)} copy(f32[256,4,1440]{0,2,1:T(8,128)} %pad_maximum_fusion) | data formatting | bytes 11796480 | tf_op jit(solution)/shard_map/concatenate | solution.py:55
  202.5 215.7 %all-reduce.6 = (bf16[256,4,1440]{2,1,0:T(4,128)(2,1)}, bf16[256,4,1440]{2,1,0:T(4,128)(2,1)}) all-reduce(f32[256,4,1440]{2,1,0:T(4,128)} %copy.63, f32[256,4,1440]{2,1,0:T(4,128)} %copy.70), channel_id=2, replica_groups=mesh['expert'=64,'dp'=4] {'dp'}, use_global_device_ids=true, to_apply=%region_6.7.clone | all-reduce | flops 2949120 | bytes 17694720
  418.2 2.3 dynamic-slice_convert_fusion.1
  420.4 12.4 %all-to-all-start.1 = ((bf16[64,4,1440]{2,1,0:T(4,128)(2,1)}), bf16[64,4,1440]{2,1,0:T(4,128)(2,1)S(1)}, u32[]{:S(2)}, u32[]{:S(2)}) async-start(bf16[64,4,1440]{2,1,0:T(4,128)(2,1)} %dynamic-slice_convert_fusion.1), calls=%async_computation.1 | async-start | bytes 1572864 | tf_op jit(solution)/shard_map/all_to_all | solution.py:123
  432.8 1.5 convolution_convert_fusion.1
  434.3 3.0 collective-permute-start.3
  437.3 2.3 dynamic-slice_convert_fusion
  439.6 16.1 %all-to-all-done.1 = bf16[64,4,1440]{2,1,0:T(4,128)(2,1)S(1)} async-done(((bf16[64,4,1440]{2,1,0:T(4,128)(2,1)}), bf16[64,4,1440]{2,1,0:T(4,128)(2,1)S(1)}, u32[]{:S(2)}, u32[]{:S(2)}) %all-to-all-start.1) | async-done | bytes 737312 | tf_op jit(solution)/shard_map/all_to_all | solution.py:123
  455.8 6.2 %all-to-all-start.3 = ((bf16[64,4,1440]{2,1,0:T(4,128)(2,1)}), bf16[64,4,1440]{2,1,0:T(4,128)(2,1)S(1)}, u32[]{:S(2)}, u32[]{:S(2)}) async-start(bf16[64,4,1440]{2,1,0:T(4,128)(2,1)} %dynamic-slice_convert_fusion), calls=%async_computation.3 | async-start | bytes 1572864 | tf_op jit(solution)/shard_map/all_to_all | solution.py:175
  462.6 3.1 collective-permute-start.2
  465.7 4.0 collective-permute-done.3
  469.7 4.0 fusion.3
  473.7 27.4 %collective-permute-done.2 = bf16[1440,360]{1,0:T(8,128)(2,1)S(1)} collective-permute-done((bf16[1440,360]{1,0:T(8,128)(2,1)S(1)}, bf16[1440,360]{1,0:T(8,128)(2,1)S(1)}, u32[]{:S(2)}, u32[]{:S(2)}) %collective-permute-start.2) | collective-permute-done | bytes 1036832 | tf_op jit(solution)/shard_map/ppermute | solution.py:10
  501.1 2.4 fusion.2
  504.4 3.2 gather_fusion.5
  507.6 2.9 gather.36
  510.5 2.2 reduce_sum.55
  513.6 3.0 gather_fusion.2
  516.6 2.9 reshape.322
  519.5 3.1 multiply_reduce_fusion
  (95 shorter events, 10.6 us)
Async XLA Ops:
  7.2 4.9 copy-start.15
  7.2 5.0 copy-start.16
  7.2 5.5 %copy-start.18 = (s32[8]{0:T(128)S(1)}, s32[8]{0:T(128)}, u32[]{:S(2)}) copy-start(s32[8]{0:T(128)} %param.14) | copy-start | bytes 100
  7.2 89.9 %all-gather.5.cloned.1.call-start = ((), (), s32[]{:S(2)}) async-start(), calls=%async_computation.5 | async-start | bytes 3932160 | tf_op jit(solution)/shard_map/all_gather | solution.py:125
  8.7 8.2 %copy-start.17 = (s32[128,4]{0,1:T(4,128)S(1)}, s32[128,4]{0,1:T(4,128)}, u32[]{:S(2)}) copy-start(s32[128,4]{0,1:T(4,128)} %param.12) | copy-start | bytes 6148
  12.1 7.3 %copy-start.13 = (bf16[128,1440]{0,1:T(8,128)(2,1)S(1)}, bf16[128,1440]{0,1:T(8,128)(2,1)}, u32[]{:S(2)}) copy-start(bf16[128,1440]{0,1:T(8,128)(2,1)} %param.17) | copy-start | bytes 1105924
  17.1 2.2 copy-start.8
  21.8 36.3 %copy-start.14 = (bf16[128,1440]{0,1:T(8,128)(2,1)S(1)}, bf16[128,1440]{0,1:T(8,128)(2,1)}, u32[]{:S(2)}) copy-start(bf16[128,1440]{0,1:T(8,128)(2,1)} %param.10) | copy-start | bytes 1105924
  58.0 83.2 %all-gather.3.cloned.1.call-start = ((), (), s32[]{:S(2)}) async-start(), calls=%async_computation.4 | async-start | bytes 3932160 | tf_op jit(solution)/shard_map/all_gather | solution.py:99
  60.1 32.2 %copy-start.19 = (u32[256]{0:T(256)S(1)}, u32[256]{0:T(256)}, u32[]{:S(2)}) copy-start(u32[256]{0:T(256)} %constant.170) | copy-start | bytes 3076
  89.2 78.8 %collective-permute-start = (bf16[1,1440,360]{2,1,0:T(8,128)(2,1)}, bf16[1,1440,360]{2,1,0:T(8,128)(2,1)}, u32[]{:S(2)}, u32[]{:S(2)}) collective-permute-start(bf16[1,1440,360]{2,1,0:T(8,128)(2,1)} %param.15), channel_id=1, source_target_pairs={{0,128},{4,132},{8,136},{12,140},{16,144},{20,148},{24,152},{28,15... | collective-permute-start | bytes 3110408 | tf_op jit(solution)/shard_map/ppermute | solution.py:10
  92.1 80.8 %collective-permute-start.1 = (bf16[1,360,1440]{2,1,0:T(8,128)(2,1)}, bf16[1,360,1440]{2,1,0:T(8,128)(2,1)}, u32[]{:S(2)}, u32[]{:S(2)}) collective-permute-start(bf16[1,360,1440]{2,1,0:T(8,128)(2,1)} %param.16), channel_id=1, source_target_pairs={{0,128},{4,132},{8,136},{12,140},{16,144},{20,148},{24,152},{28,15... | collective-permute-start | bytes 3110408 | tf_op jit(solution)/shard_map/ppermute | solution.py:10
  141.2 9.5 %copy-start = (bf16[256,4,1440]{2,1,0:T(4,128)(2,1)S(1)}, bf16[256,4,1440]{2,1,0:T(4,128)(2,1)}, u32[]{:S(2)}) copy-start(bf16[256,4,1440]{2,1,0:T(4,128)(2,1)} %all-gather.5.cloned.1.call-done) | copy-start | bytes 8847364
  160.2 3.3 copy-start.2
  160.2 3.4 copy-start.4
  163.5 3.0 copy-start.11
  166.2 0.8 copy-start.9
  167.3 1.1 copy-start.1
  170.2 2.7 copy-start.5
  174.6 4.8 copy-start.6
  420.4 35.3 %all-to-all-start.1 = ((bf16[64,4,1440]{2,1,0:T(4,128)(2,1)}), bf16[64,4,1440]{2,1,0:T(4,128)(2,1)S(1)}, u32[]{:S(2)}, u32[]{:S(2)}) async-start(bf16[64,4,1440]{2,1,0:T(4,128)(2,1)} %dynamic-slice_convert_fusion.1), calls=%async_computation.1 | async-start | bytes 1572864 | tf_op jit(solution)/shard_map/all_to_all | solution.py:123
  434.3 35.4 %collective-permute-start.3 = (bf16[360,1440]{1,0:T(8,128)(2,1)}, bf16[360,1440]{1,0:T(8,128)(2,1)}, u32[]{:S(2)}, u32[]{:S(2)}) collective-permute-start(bf16[360,1440]{1,0:T(8,128)(2,1)} %convolution_convert_fusion.1), channel_id=1, source_target_pairs={{0,128},{4,132},{8,136},{12,140},{16,144},{20,148},{24,152},{28,15... | collective-permute-start | bytes 3110408 | tf_op jit(solution)/shard_map/ppermute | solution.py:10
  437.3 24.7 %copy-start.7 = (bf16[256,360]{0,1:T(8,128)(2,1)S(1)}, bf16[256,360]{0,1:T(8,128)(2,1)}, u32[]{:S(2)}) copy-start(bf16[256,360]{0,1:T(8,128)(2,1)} %copy-done.6) | copy-start | bytes 552964
  439.6 30.0 %copy-start.12 = (bf16[768,360]{0,1:T(8,128)(2,1)S(1)}, bf16[768,360]{0,1:T(8,128)(2,1)}, u32[]{:S(2)}) copy-start(bf16[768,360]{0,1:T(8,128)(2,1)} %copy-done.11) | copy-start | bytes 1658884
  455.8 48.2 %all-to-all-start.3 = ((bf16[64,4,1440]{2,1,0:T(4,128)(2,1)}), bf16[64,4,1440]{2,1,0:T(4,128)(2,1)S(1)}, u32[]{:S(2)}, u32[]{:S(2)}) async-start(bf16[64,4,1440]{2,1,0:T(4,128)(2,1)} %dynamic-slice_convert_fusion), calls=%async_computation.3 | async-start | bytes 1572864 | tf_op jit(solution)/shard_map/all_to_all | solution.py:175
  462.6 38.5 %collective-permute-start.2 = (bf16[1440,360]{1,0:T(8,128)(2,1)S(1)}, bf16[1440,360]{1,0:T(8,128)(2,1)S(1)}, u32[]{:S(2)}, u32[]{:S(2)}) collective-permute-start(bf16[1440,360]{1,0:T(8,128)(2,1)S(1)} %convolution_convert_fusion), channel_id=1, source_target_pairs={{0,128},{4,132},{8,136},{12,140},{16,144},{20,148},{24,152},{28,15... | collective-permute-start | bytes 3110408 | tf_op jit(solution)/shard_map/ppermute | solution.py:10
  465.7 35.4 %copy-start.3 = (bf16[768,1440]{1,0:T(8,128)(2,1)S(1)}, bf16[768,1440]{1,0:T(8,128)(2,1)}, u32[]{:S(2)}) copy-start(bf16[768,1440]{1,0:T(8,128)(2,1)} %copy-done.2) | copy-start | bytes 6635524
  465.7 35.4 %copy-start.10 = (bf16[768,360]{0,1:T(8,128)(2,1)S(1)}, bf16[768,360]{0,1:T(8,128)(2,1)}, u32[]{:S(2)}) copy-start(bf16[768,360]{0,1:T(8,128)(2,1)} %copy-done.9) | copy-start | bytes 1658884
Sparse Core Ops, SparseCore 0:
  58.1 38.9 all-gather.4
  98.9 42.2 all-gather.2
where the time goes:
time: 540 us; the launch traced here: 531 us
  blocking collectives  281 us (52%)
  waiting for transfers between devices  88.3 us (16%)
  local copies, waits for them, and re-layouts  76.1 us (14%)
  starting transfers between devices  27.8 us (5%)
  matrix products  27 us (5%)
  between operations  16.2 us (3%)
  other arithmetic  14.4 us (3%)
    unnamed x1, blocking collectives  216 us
    all_gather x1, waiting for transfers between devices, on_device(): all_in = lax.all_gather(inbound, 'dp', axis=0, tiled=True)  37.2 us
    all_to_all x1, blocking collectives, on_device(): lax.all_to_all(grad_rows, 'expert', split_axis=0, concat_axis=0, tiled=True)  36.2 us
    ppermute x4, waiting for transfers between devices, shifted(): return lax.ppermute(value, axis, pairs)  31.4 us
    all_to_all x1, blocking collectives, on_device(): lax.all_to_all(sent_rows, 'expert', split_axis=0, concat_axis=0, tiled=True)  29.1 us
    all_to_all x1, waiting for transfers between devices, on_device(): lax.all_to_all(outputs, 'expert', split_axis=0, concat_axis=0, tiled=True)  16.1 us
    concatenate x2, local copies, waits for them, and re-layouts, slot_products(): jnp.concatenate([own_term.reshape(amount, capacity, -1), copy_term.reshap...  15.7 us
    all_to_all x1, starting transfers between devices, on_device(): lax.all_to_all(outputs, 'expert', split_axis=0, concat_axis=0, tiled=True)  12.4 us
  transfers between devices with their start and end apart: 8, of which 5 were waited for; matrix products, arithmetic and copies ran while one was open for 10% of the time, Pallas kernels for 0%

commit v1 on v0

--- a/solution.py
+++ b/solution.py
@@ -96,7 +96,12 @@
     copy_first = slab_in[0]
     copy_second = slab_out[0]
     inbound = lax.all_to_all(sent_rows, "expert", split_axis=0, concat_axis=0, tiled=True)
-    all_in = lax.all_gather(inbound, "dp", axis=0, tiled=True)
+    ring = [inbound]
+    for hop in range(3):
+        ring.append(lax.ppermute(ring[-1], "dp", [(dev, (dev + 1) % 4) for dev in range(4)]))
+    all_in = jnp.roll(
+        jnp.concatenate(ring[::-1], axis=0), (lax.axis_index("dp") + 1) * ring[0].shape[0], axis=0
+    )
     blocks = all_in.shape[0]
     own_rows = all_in[:, :capacity].reshape(-1, features)
     copy_rows = all_in[:, capacity:].reshape(-1, features)

time: 540 us -> 527 us (0.976)
  blocking collectives: 281 us -> 214 us
  waiting for transfers between devices: 88.3 us -> 115 us
  starting transfers between devices: 27.8 us -> 47.3 us
  local copies, waits for them, and re-layouts: 76.1 us -> 82.4 us
    all_to_all x2 -> x0, blocking collectives: 65.3 us -> none  [the longest x1 36.2 us: on_device(): lax.all_to_all(grad_rows, 'expert', split_axis=0, concat_axis=0, tiled=True)]
    ppermute x0 -> x3, waiting for transfers between devices: none -> 39.8 us  [on_device(): lax.ppermute(ring[-1], 'dp', [(dev, (dev + 1) % 4) for dev in range(4)])]
    all_gather x1 -> x0, waiting for transfers between devices: 37.2 us -> none  [on_device(): all_in = lax.all_gather(inbound, 'dp', axis=0, tiled=True)]
    all_to_all x0 -> x2, waiting for transfers between devices: none -> 21 us  [the longest x1 21 us: on_device(): lax.all_to_all(sent_rows, 'expert', split_axis=0, concat_axis=0, tiled=True)]
    all_to_all x0 -> x2, starting transfers between devices: none -> 19.8 us  [the longest x1 13.2 us: on_device(): lax.all_to_all(sent_rows, 'expert', split_axis=0, concat_axis=0, tiled=True)]
    all_to_all x1, waiting for transfers between devices: 16.1 us -> 0.01 us  [on_device(): lax.all_to_all(outputs, 'expert', split_axis=0, concat_axis=0, tiled=True)]
    all_to_all x1, waiting for transfers between devices: 0.01 us -> 16.1 us  [on_device(): lax.all_to_all(input_rows, 'expert', split_axis=0, concat_axis=0, tiled=T...]
    ppermute x4, waiting for transfers between devices: 31.4 us -> 38.5 us  [shifted(): return lax.ppermute(value, axis, pairs)]
  transfers between devices with their start and end apart: 8 -> 12, of which waited for: 5 -> 8; matrix products, arithmetic and copies ran while one was open for 10% -> 12% of each run, Pallas kernels for 0% -> 0%
where the time goes in v1:
time: 527 us; the launch traced here: 517 us
  blocking collectives  214 us (41%)
  waiting for transfers between devices  115 us (22%)
  local copies, waits for them, and re-layouts  82.4 us (16%)
  starting transfers between devices  47.3 us (9%)
  matrix products  25.9 us (5%)
  between operations  16.3 us (3%)
  other arithmetic  16.1 us (3%)
    unnamed x1, blocking collectives  214 us
    ppermute x3, waiting for transfers between devices, on_device(): lax.ppermute(ring[-1], 'dp', [(dev, (dev + 1) % 4) for dev in range(4)])  39.8 us
    ppermute x4, waiting for transfers between devices, shifted(): return lax.ppermute(value, axis, pairs)  38.5 us
    all_to_all x1, waiting for transfers between devices, on_device(): lax.all_to_all(sent_rows, 'expert', split_axis=0, concat_axis=0, tiled=True)  21 us
    unnamed x54, local copies, waits for them, and re-layouts  16.8 us
    all_to_all x1, waiting for transfers between devices, on_device(): lax.all_to_all(input_rows, 'expert', split_axis=0, concat_axis=0, tiled=T...  16.1 us
    concatenate x2, local copies, waits for them, and re-layouts, slot_products(): jnp.concatenate([own_term.reshape(amount, capacity, -1), copy_term.reshap...  15.8 us
    all_to_all x1, starting transfers between devices, on_device(): lax.all_to_all(sent_rows, 'expert', split_axis=0, concat_axis=0, tiled=True)  13.2 us
  transfers between devices with their start and end apart: 12, of which 8 were waited for; matrix products, arithmetic and copies ran while one was open for 12% of the time, Pallas kernels for 0%

profile of v1, /device:TPU:1, one launch (start us, length us, event | category | flops | bytes accessed | tf_op | source)
XLA Modules:
  0.0 517.4 jit_solution(2913279683939426923)
XLA Ops:
  8.7 3.3 gather_fusion
  14.4 2.4 scatter_custom_fusion
  20.0 13.2 %all-to-all-start = ((bf16[64,4,1440]{2,1,0:T(4,128)(2,1)}), bf16[64,4,1440]{2,1,0:T(4,128)(2,1)S(1)}, u32[]{:S(2)}, u32[]{:S(2)}) async-start(bf16[64,4,1440]{2,1,0:T(4,128)(2,1)} %broadcast_select_fusion), calls=%async_computation | async-start | bytes 1572864 | tf_op jit(solution)/shard_map/all_to_all | solution.py:98
  35.2 21.0 %all-to-all-done = bf16[64,4,1440]{2,1,0:T(4,128)(2,1)S(1)} async-done(((bf16[64,4,1440]{2,1,0:T(4,128)(2,1)}), bf16[64,4,1440]{2,1,0:T(4,128)(2,1)S(1)}, u32[]{:S(2)}, u32[]{:S(2)}) %all-to-all-start) | async-done | bytes 737312 | tf_op jit(solution)/shard_map/all_to_all | solution.py:98
  57.6 1.9 gather_fusion.3
  61.0 6.6 %all-to-all-start.2 = ((bf16[64,4,1440]{2,1,0:T(4,128)(2,1)}), bf16[64,4,1440]{2,1,0:T(4,128)(2,1)S(1)}, u32[]{:S(2)}, u32[]{:S(2)}) async-start(bf16[64,4,1440]{2,1,0:T(4,128)(2,1)} %select_convert_fusion), calls=%async_computation.2 | async-start | bytes 1572864 | tf_op jit(solution)/shard_map/all_to_all | solution.py:129
  67.7 8.4 %collective-permute-done = bf16[64,4,1440]{2,1,0:T(4,128)(2,1)S(1)} collective-permute-done((bf16[64,4,1440]{2,1,0:T(4,128)(2,1)S(1)}, bf16[64,4,1440]{2,1,0:T(4,128)(2,1)S(1)}, u32[]{:S(2)}, u32[]{:S(2)}) %collective-permute-start) | collective-permute-done | bytes 737312 | tf_op jit(solution)/shard_map/ppermute | solution.py:101
  76.1 19.0 %collective-permute-done.1 = bf16[64,4,1440]{2,1,0:T(4,128)(2,1)S(1)} collective-permute-done((bf16[64,4,1440]{2,1,0:T(4,128)(2,1)S(1)}, bf16[64,4,1440]{2,1,0:T(4,128)(2,1)S(1)}, u32[]{:S(2)}, u32[]{:S(2)}) %collective-permute-start.1) | collective-permute-done | bytes 737312 | tf_op jit(solution)/shard_map/ppermute | solution.py:101
  96.0 4.7 collective-permute-start.3
  102.2 12.3 %collective-permute-done.2 = bf16[64,4,1440]{2,1,0:T(4,128)(2,1)} collective-permute-done((bf16[64,4,1440]{2,1,0:T(4,128)(2,1)S(1)}, bf16[64,4,1440]{2,1,0:T(4,128)(2,1)}, u32[]{:S(2)}, u32[]{:S(2)}) %collective-permute-start.2) | collective-permute-done | bytes 737312 | tf_op jit(solution)/shard_map/ppermute | solution.py:101
  119.4 2.6 copy-done.3
  122.0 1.6 constant_dynamic-slice_fusion.1
  123.6 2.9 copy.62
  126.5 3.0 constant_dynamic-slice_fusion
  129.5 4.2 reshape.314
  133.7 4.1 multiply_convert_fusion
  139.2 1.8 fusion.12
  141.1 7.2 %collective-permute-done.4 = bf16[1,360,1440]{2,1,0:T(8,128)(2,1)} collective-permute-done((bf16[1,360,1440]{2,1,0:T(8,128)(2,1)}, bf16[1,360,1440]{2,1,0:T(8,128)(2,1)}, u32[]{:S(2)}, u32[]{:S(2)}) %collective-permute-start.4) | collective-permute-done | bytes 1036832 | tf_op jit(solution)/shard_map/ppermute | solution.py:10
  148.3 1.9 convolution_bitcast_fusion.1
  151.6 2.9 pad_maximum_fusion
  154.5 8.0 %copy.63 = f32[256,4,1440]{2,1,0:T(4,128)} copy(f32[256,4,1440]{0,2,1:T(8,128)} %pad_maximum_fusion) | data formatting | bytes 11796480 | tf_op jit(solution)/shard_map/concatenate | solution.py:55
  162.4 4.9 slice.58
  167.3 4.6 copy.75
  171.9 4.1 reshape.318
  176.0 3.5 fusion.2
  182.1 1.7 fusion.3
  183.8 1.8 convolution_bitcast_fusion
  185.6 2.8 pad_maximum_fusion.1
  188.4 7.9 %copy.70 = f32[256,4,1440]{2,1,0:T(4,128)} copy(f32[256,4,1440]{0,2,1:T(8,128)} %pad_maximum_fusion.1) | data formatting | bytes 11796480 | tf_op jit(solution)/shard_map/concatenate | solution.py:55
  196.3 213.9 %all-reduce.6 = (bf16[256,4,1440]{2,1,0:T(4,128)(2,1)}, bf16[256,4,1440]{2,1,0:T(4,128)(2,1)}) all-reduce(f32[256,4,1440]{2,1,0:T(4,128)} %copy.63, f32[256,4,1440]{2,1,0:T(4,128)} %copy.70), channel_id=2, replica_groups=mesh['expert'=64,'dp'=4] {'dp'}, use_global_device_ids=true, to_apply=%region_6.7.clone | all-reduce | flops 2949120 | bytes 17694720
  410.2 2.4 dynamic-slice_convert_fusion
  412.6 8.9 %all-to-all-start.3 = ((bf16[64,4,1440]{2,1,0:T(4,128)(2,1)}), bf16[64,4,1440]{2,1,0:T(4,128)(2,1)S(1)}, u32[]{:S(2)}, u32[]{:S(2)}) async-start(bf16[64,4,1440]{2,1,0:T(4,128)(2,1)} %dynamic-slice_convert_fusion), calls=%async_computation.3 | async-start | bytes 1572864 | tf_op jit(solution)/shard_map/all_to_all | solution.py:180
  421.5 1.5 convolution_convert_fusion.1
  422.9 3.0 collective-permute-start.6
  425.9 2.4 dynamic-slice_convert_fusion.1
  428.3 16.1 %all-to-all-done.3 = bf16[64,4,1440]{2,1,0:T(4,128)(2,1)S(1)} async-done(((bf16[64,4,1440]{2,1,0:T(4,128)(2,1)}), bf16[64,4,1440]{2,1,0:T(4,128)(2,1)S(1)}, u32[]{:S(2)}, u32[]{:S(2)}) %all-to-all-start.3) | async-done | bytes 737312 | tf_op jit(solution)/shard_map/all_to_all | solution.py:180
  444.4 6.4 %all-to-all-start.1 = ((bf16[64,4,1440]{2,1,0:T(4,128)(2,1)}), bf16[64,4,1440]{2,1,0:T(4,128)(2,1)}, u32[]{:S(2)}, u32[]{:S(2)}) async-start(bf16[64,4,1440]{2,1,0:T(4,128)(2,1)} %dynamic-slice_convert_fusion.1), calls=%async_computation.1 | async-start | bytes 1572864 | tf_op jit(solution)/shard_map/all_to_all | solution.py:128
  451.4 3.1 collective-permute-start.5
  454.5 3.8 collective-permute-done.6
  458.3 4.0 fusion.4
  462.3 27.4 %collective-permute-done.5 = bf16[1440,360]{1,0:T(8,128)(2,1)S(1)} collective-permute-done((bf16[1440,360]{1,0:T(8,128)(2,1)S(1)}, bf16[1440,360]{1,0:T(8,128)(2,1)S(1)}, u32[]{:S(2)}, u32[]{:S(2)}) %collective-permute-start.5) | collective-permute-done | bytes 1036832 | tf_op jit(solution)/shard_map/ppermute | solution.py:10
  489.7 2.5 fusion.1
  492.6 2.4 gather_fusion.5
  495.4 2.1 reduce_sum.55
  498.5 1.6 reshape.317
  500.1 3.0 gather_fusion.2
  503.1 2.9 reshape.322
  506.0 3.1 multiply_reduce_fusion
  (109 shorter events, 26.4 us)
Async XLA Ops:
  7.2 4.9 copy-start.15
  7.2 5.0 copy-start.16
  7.2 7.0 %copy-start.18 = (s32[8]{0:T(128)S(1)}, s32[8]{0:T(128)}, u32[]{:S(2)}) copy-start(s32[8]{0:T(128)} %param.14) | copy-start | bytes 100
  7.2 9.7 %copy-start.13 = (bf16[128,1440]{0,1:T(8,128)(2,1)S(1)}, bf16[128,1440]{0,1:T(8,128)(2,1)}, u32[]{:S(2)}) copy-start(bf16[128,1440]{0,1:T(8,128)(2,1)} %param.10) | copy-start | bytes 1105924
  18.7 14.5 %copy-start.14 = (bf16[128,1440]{0,1:T(8,128)(2,1)S(1)}, bf16[128,1440]{0,1:T(8,128)(2,1)}, u32[]{:S(2)}) copy-start(bf16[128,1440]{0,1:T(8,128)(2,1)} %param.17) | copy-start | bytes 1105924
  20.0 36.1 %all-to-all-start = ((bf16[64,4,1440]{2,1,0:T(4,128)(2,1)}), bf16[64,4,1440]{2,1,0:T(4,128)(2,1)S(1)}, u32[]{:S(2)}, u32[]{:S(2)}) async-start(bf16[64,4,1440]{2,1,0:T(4,128)(2,1)} %broadcast_select_fusion), calls=%async_computation | async-start | bytes 1572864 | tf_op jit(solution)/shard_map/all_to_all | solution.py:98
  34.6 22.7 %copy-start.17 = (s32[128,4]{0,1:T(4,128)S(1)}, s32[128,4]{0,1:T(4,128)}, u32[]{:S(2)}) copy-start(s32[128,4]{0,1:T(4,128)} %param.12) | copy-start | bytes 6148
  56.2 19.9 %collective-permute-start = (bf16[64,4,1440]{2,1,0:T(4,128)(2,1)S(1)}, bf16[64,4,1440]{2,1,0:T(4,128)(2,1)S(1)}, u32[]{:S(2)}, u32[]{:S(2)}) collective-permute-start(bf16[64,4,1440]{2,1,0:T(4,128)(2,1)S(1)} %all-to-all-done), channel_id=1, source_target_pairs={{0,1},{1,2},{2,3},{3,0},{4,5},{5,6},{6,7},{7,4},{8,9},{9,10},{10,1... | collective-permute-start | bytes 2211848 | tf_op jit(solution)/shard_map/ppermute | solution.py:101
  57.5 3.5 copy-start.10
  61.0 40.0 %copy-start.19 = (u32[256]{0:T(256)S(1)}, u32[256]{0:T(256)}, u32[]{:S(2)}) copy-start(u32[256]{0:T(256)} %constant.195) | copy-start | bytes 3076
  61.0 34.1 %all-to-all-start.2 = ((bf16[64,4,1440]{2,1,0:T(4,128)(2,1)}), bf16[64,4,1440]{2,1,0:T(4,128)(2,1)S(1)}, u32[]{:S(2)}, u32[]{:S(2)}) async-start(bf16[64,4,1440]{2,1,0:T(4,128)(2,1)} %select_convert_fusion), calls=%async_computation.2 | async-start | bytes 1572864 | tf_op jit(solution)/shard_map/all_to_all | solution.py:129
  67.6 94.8 %all-gather.2.cloned.1.call-start = ((), (), s32[]{:S(2)}) async-start(), calls=%async_computation.4 | async-start | bytes 3932160 | tf_op jit(solution)/shard_map/all_gather | solution.py:130
  76.1 19.0 %collective-permute-start.1 = (bf16[64,4,1440]{2,1,0:T(4,128)(2,1)S(1)}, bf16[64,4,1440]{2,1,0:T(4,128)(2,1)S(1)}, u32[]{:S(2)}, u32[]{:S(2)}) collective-permute-start(bf16[64,4,1440]{2,1,0:T(4,128)(2,1)S(1)} %collective-permute-done), channel_id=1, source_target_pairs={{0,1},{1,2},{2,3},{3,0},{4,5},{5,6},{6,7},{7,4},{8,9},{9,10},{10,1... | collective-permute-start | bytes 2211848 | tf_op jit(solution)/shard_map/ppermute | solution.py:101
  95.1 19.4 %collective-permute-start.2 = (bf16[64,4,1440]{2,1,0:T(4,128)(2,1)S(1)}, bf16[64,4,1440]{2,1,0:T(4,128)(2,1)}, u32[]{:S(2)}, u32[]{:S(2)}) collective-permute-start(bf16[64,4,1440]{2,1,0:T(4,128)(2,1)S(1)} %collective-permute-done.1), channel_id=1, source_target_pairs={{0,1},{1,2},{2,3},{3,0},{4,5},{5,6},{6,7},{7,4},{8,9},{9,10},{10,1... | collective-permute-start | bytes 2211848 | tf_op jit(solution)/shard_map/ppermute | solution.py:101
  95.1 0.9 copy-start.4
  96.0 43.2 %collective-permute-start.3 = (bf16[1,1440,360]{2,1,0:T(8,128)(2,1)}, bf16[1,1440,360]{2,1,0:T(8,128)(2,1)}, u32[]{:S(2)}, u32[]{:S(2)}) collective-permute-start(bf16[1,1440,360]{2,1,0:T(8,128)(2,1)} %param.15), channel_id=1, source_target_pairs={{0,128},{4,132},{8,136},{12,140},{16,144},{20,148},{24,152},{28,15... | collective-permute-start | bytes 3110408 | tf_op jit(solution)/shard_map/ppermute | solution.py:10
  100.7 47.6 %collective-permute-start.4 = (bf16[1,360,1440]{2,1,0:T(8,128)(2,1)}, bf16[1,360,1440]{2,1,0:T(8,128)(2,1)}, u32[]{:S(2)}, u32[]{:S(2)}) collective-permute-start(bf16[1,360,1440]{2,1,0:T(8,128)(2,1)} %param.16), channel_id=1, source_target_pairs={{0,128},{4,132},{8,136},{12,140},{16,144},{20,148},{24,152},{28,15... | collective-permute-start | bytes 3110408 | tf_op jit(solution)/shard_map/ppermute | solution.py:10
  119.3 2.7 copy-start.3
  137.8 0.8 copy-start.11
  137.8 1.5 copy-start.1
  141.1 9.1 %copy-start.6 = (bf16[1,360,1440]{2,1,0:T(8,128)(2,1)S(1)}, bf16[1,360,1440]{2,1,0:T(8,128)(2,1)}, u32[]{:S(2)}) copy-start(bf16[1,360,1440]{2,1,0:T(8,128)(2,1)} %param.16) | copy-start | bytes 3110404
  162.4 9.5 %copy-start = (bf16[256,4,1440]{2,1,0:T(4,128)(2,1)S(1)}, bf16[256,4,1440]{2,1,0:T(4,128)(2,1)}, u32[]{:S(2)}) copy-start(bf16[256,4,1440]{2,1,0:T(4,128)(2,1)} %all-gather.2.cloned.1.call-done) | copy-start | bytes 8847364
  179.5 1.2 copy-start.7
  180.7 1.3 copy-start.8
  410.2 11.2 %copy-start.9 = (bf16[256,1,1440]{0,2,1:T(8,128)(2,1)S(1)}, bf16[256,1,1440]{0,2,1:T(8,128)(2,1)}, u32[]{:S(2)}) copy-start(bf16[256,1,1440]{0,2,1:T(8,128)(2,1)} %copy.75) | copy-start | bytes 2211844
  412.6 31.9 %all-to-all-start.3 = ((bf16[64,4,1440]{2,1,0:T(4,128)(2,1)}), bf16[64,4,1440]{2,1,0:T(4,128)(2,1)S(1)}, u32[]{:S(2)}, u32[]{:S(2)}) async-start(bf16[64,4,1440]{2,1,0:T(4,128)(2,1)} %dynamic-slice_convert_fusion), calls=%async_computation.3 | async-start | bytes 1572864 | tf_op jit(solution)/shard_map/all_to_all | solution.py:180
  422.9 35.4 %collective-permute-start.6 = (bf16[360,1440]{1,0:T(8,128)(2,1)}, bf16[360,1440]{1,0:T(8,128)(2,1)}, u32[]{:S(2)}, u32[]{:S(2)}) collective-permute-start(bf16[360,1440]{1,0:T(8,128)(2,1)} %convolution_convert_fusion.1), channel_id=1, source_target_pairs={{0,128},{4,132},{8,136},{12,140},{16,144},{20,148},{24,152},{28,15... | collective-permute-start | bytes 3110408 | tf_op jit(solution)/shard_map/ppermute | solution.py:10
  425.9 24.9 %copy-start.2 = (bf16[256,1,1440]{0,2,1:T(8,128)(2,1)S(1)}, bf16[256,1,1440]{0,2,1:T(8,128)(2,1)}, u32[]{:S(2)}) copy-start(bf16[256,1,1440]{0,2,1:T(8,128)(2,1)} %copy.62) | copy-start | bytes 2211844
  428.3 30.0 %copy-start.12 = (bf16[768,360]{0,1:T(8,128)(2,1)S(1)}, bf16[768,360]{0,1:T(8,128)(2,1)}, u32[]{:S(2)}) copy-start(bf16[768,360]{0,1:T(8,128)(2,1)} %copy-done.11) | copy-start | bytes 1658884
  444.4 54.1 %all-to-all-start.1 = ((bf16[64,4,1440]{2,1,0:T(4,128)(2,1)}), bf16[64,4,1440]{2,1,0:T(4,128)(2,1)}, u32[]{:S(2)}, u32[]{:S(2)}) async-start(bf16[64,4,1440]{2,1,0:T(4,128)(2,1)} %dynamic-slice_convert_fusion.1), calls=%async_computation.1 | async-start | bytes 1572864 | tf_op jit(solution)/shard_map/all_to_all | solution.py:128
  451.4 38.3 %collective-permute-start.5 = (bf16[1440,360]{1,0:T(8,128)(2,1)S(1)}, bf16[1440,360]{1,0:T(8,128)(2,1)S(1)}, u32[]{:S(2)}, u32[]{:S(2)}) collective-permute-start(bf16[1440,360]{1,0:T(8,128)(2,1)S(1)} %convolution_convert_fusion), channel_id=1, source_target_pairs={{0,128},{4,132},{8,136},{12,140},{16,144},{20,148},{24,152},{28,15... | collective-permute-start | bytes 3110408 | tf_op jit(solution)/shard_map/ppermute | solution.py:10
  454.5 35.2 %copy-start.5 = (bf16[768,1440]{1,0:T(8,128)(2,1)S(1)}, bf16[768,1440]{1,0:T(8,128)(2,1)}, u32[]{:S(2)}) copy-start(bf16[768,1440]{1,0:T(8,128)(2,1)} %reshape.314) | copy-start | bytes 6635524
Sparse Core Ops, SparseCore 0:
  96.1 45.3 all-gather.1
